TPU v7x, 128 devices: a whole 4x4x4 slice. The times are simulated.
128 devices in a mesh: clip: 32 (over z, x, core), grp: 4 (over y).
Axes of the slice: x: 4, y: 4, z: 4, core: 2. Of those that a mesh axis runs over, the one named last changes fastest.
Arguments:
- hidden: bfloat16 [32, 20, 256, 1152], P('clip', 'grp'), may hold values from -6 to 6
- modulation: float32 [32, 3, 1152], P('clip'), may hold values from -3 to 3
- clip_frames: int32 [32], P('clip'), may hold values from 1 to 20, as said below
- qkv_weight: bfloat16 [1152, 3456], P(None, ('clip', 'grp')), may hold values from -0.1875 to 0.1875
- out_weight: bfloat16 [1152, 1152], P(None, ('clip', 'grp')), may hold values from -0.1875 to 0.1875
Outputs:
- output: bfloat16 [32, 20, 256, 1152], P('clip', 'grp')
Inputs may be any that keep to these rules, and one draw needn't show every extreme that they name: `clip_frames`: at least one clip has all 20 frames.
All inputs are finite; a program needn't handle non-finite values.
Results may differ from a plain program's by a relative error of at most 0.0085.
Values may be sent and summed in bfloat16 or wider, within the bound.
No kernel may reach another device: no remote copies, remote signals or barrier semaphores. Data moves between devices by JAX's collectives and lax.ppermute only.
A program may use at most 128 MiB of HBM per device.

v0:
```python
import jax
import jax.numpy as jnp
from jax import lax
from jax.sharding import PartitionSpec as P

HEADS = 16


def modulate(features, table):
    average = jnp.mean(features, axis=-1, keepdims=True)
    centred = features - average
    variance = jnp.mean(centred * centred, axis=-1, keepdims=True)
    normed = centred * lax.rsqrt(variance + 1e-06)
    return (normed * (1.0 + table[1]) + table[0]).astype(jnp.bfloat16)


def on_device(hidden, modulation, clip_frames, qkv_weight, out_weight):
    own_frames = hidden.shape[1]
    frame_tokens = hidden.shape[2]
    model_width = hidden.shape[3]
    group_size = lax.axis_size("grp")
    total_frames = own_frames * group_size
    cell_count = frame_tokens // group_size
    head_count = HEADS
    head_width = model_width // head_count
    table = modulation[0]
    length = clip_frames[0]
    features = hidden[0].astype(jnp.float32)
    modulated = modulate(features, table)
    frame_rows = modulated.reshape(own_frames * frame_tokens, model_width)
    qkv_rows = jnp.dot(
        frame_rows,
        lax.all_gather(qkv_weight, ("clip", "grp"), axis=1, tiled=True),
        preferred_element_type=jnp.float32,
    ).astype(jnp.bfloat16)
    qkv_rows = qkv_rows.reshape(own_frames, frame_tokens, 3 * model_width)
    qkv_rows = lax.all_to_all(qkv_rows, "grp", split_axis=1, concat_axis=0, tiled=True)
    query_heads = qkv_rows[:, :, :model_width].reshape(
        total_frames, cell_count, head_count, head_width
    )
    key_heads = qkv_rows[:, :, model_width : 2 * model_width].reshape(
        total_frames, cell_count, head_count, head_width
    )
    value_heads = qkv_rows[:, :, 2 * model_width :].reshape(
        total_frames, cell_count, head_count, head_width
    )
    scores = jnp.einsum(
        "fshd,gshd->hfgs", query_heads, key_heads, preferred_element_type=jnp.float32
    ) * head_width ** (-0.5)
    key_live = jnp.arange(total_frames) < length
    scores = jnp.where(key_live[None, None, :, None], scores, -1e30)
    attn_weights = jax.nn.softmax(scores, axis=2).astype(jnp.bfloat16)
    mixed = jnp.einsum(
        "hfgs,gshd->fshd", attn_weights, value_heads, preferred_element_type=jnp.float32
    ).astype(jnp.bfloat16)
    mixed = mixed.reshape(total_frames, cell_count, model_width)
    returned = lax.all_to_all(mixed, "grp", split_axis=0, concat_axis=1, tiled=True)
    attn_rows = returned.reshape(own_frames * frame_tokens, model_width)
    first_frame = lax.axis_index("grp") * own_frames
    frame_live = (first_frame + jnp.arange(own_frames) < length).astype(jnp.float32)
    gate_row = table[2]
    block_cols = lax.all_gather(out_weight, ("clip", "grp"), axis=1, tiled=True)
    col_count = block_cols.shape[1]
    projected = jnp.dot(attn_rows, block_cols, preferred_element_type=jnp.float32).reshape(
        own_frames, frame_tokens, col_count
    )
    result = (features + gate_row * projected * frame_live[:, None, None]).astype(jnp.bfloat16)
    return result[None]


def solution(mesh):
    placed = (
        P("clip", "grp", None, None),
        P("clip", None, None),
        P("clip"),
        P(None, ("clip", "grp")),
        P(None, ("clip", "grp")),
    )
    return jax.shard_map(
        on_device,
        mesh=mesh,
        in_specs=placed,
        out_specs=P("clip", "grp", None, None),
        check_vma=False,
    )
```

profile of v0, /device:TPU:0, one launch (start us, length us, event | category | flops | bytes accessed | tf_op | source)
XLA Modules:
  0.0 465.9 jit_solution(11102783099813035561)
XLA Ops:
  6.5 0.0 copy-start
  6.5 0.0 copy-start.2
  6.5 0.0 all-gather.5.cloned.1.call-start
  6.5 0.7 all-gather.5.cloned.1.call-update
  7.3 2.4 convert_reduce_fusion
  9.7 2.8 fusion.19
  12.5 0.0 copy-done.2
  12.5 0.0 copy-done
  12.5 2.7 fusion.17
  15.3 68.5 %all-gather.5.cloned.1.call-done = bf16[128,27,1152]{2,1,0:T(8,128)(2,1)} async-done(((bf16[1,27,1152]{2,1,0:T(8,128)(2,1)}), bf16[128,27,1152]{2,1,0:T(8,128)(2,1)}) %all-gather.5.cloned.1.call-update) | async-done | bytes 7962640 | tf_op jit(solution)/shard_map/all_gather | solution.py:33
  83.7 13.1 %reshape.75 = bf16[3456,1152]{1,0:T(8,128)(2,1)} reshape(bf16[128,27,1152]{2,1,0:T(8,128)(2,1)} %all-gather.5.cloned.1.call-done) | data formatting | bytes 15925248
  96.8 18.0 %convolution_convert_fusion = bf16[1280,3456]{1,0:T(8,128)(2,1)} fusion(bf16[1280,1152]{1,0:T(8,128)(2,1)} %fusion.17, bf16[3456,1152]{1,0:T(8,128)(2,1)} %reshape.75), kind=kOutput, calls=%fused_computation.1 | convolution fusion | flops 10196582400 | bytes 19759104 | tf_op jit(solution)/shard_map/dot_general | solution.py:31
  114.8 13.5 %copy.20 = bf16[5,256,3456]{2,0,1:T(8,128)(2,1)} copy(bf16[5,256,3456]{2,1,0:T(8,128)(2,1)} %bitcast.61) | data formatting | bytes 17694720 | tf_op jit(solution)/shard_map/reshape | solution.py:36
  128.3 6.5 %all-to-all-start = ((bf16[5,256,3456]{2,0,1:T(8,128)(2,1)}), bf16[5,256,3456]{2,0,1:T(8,128)(2,1)}, u32[]{:S(2)}, u32[]{:S(2)}) async-start(bf16[5,256,3456]{2,0,1:T(8,128)(2,1)} %copy.20), calls=%async_computation | async-start | bytes 28311552 | tf_op jit(solution)/shard_map/all_to_all | solution.py:37
  134.8 0.3 all-gather.7.cloned.1.call-start
  135.1 0.4 all-gather.7.cloned.1.call-update
  136.2 163.2 %all-to-all-done = bf16[5,256,3456]{2,0,1:T(8,128)(2,1)} async-done(((bf16[5,256,3456]{2,0,1:T(8,128)(2,1)}), bf16[5,256,3456]{2,0,1:T(8,128)(2,1)}, u32[]{:S(2)}, u32[]{:S(2)}) %all-to-all-start) | async-done | bytes 8847392 | tf_op jit(solution)/shard_map/all_to_all | solution.py:37
  299.4 6.9 %copy.22 = bf16[4,5,64,3456]{3,2,1,0:T(8,128)(2,1)S(1)} copy(bf16[4,5,64,3456]{3,1,2,0:T(8,128)(2,1)} %bitcast.7) | data formatting | bytes 17694720 | tf_op jit(solution)/shard_map/all_to_all | solution.py:37
  306.3 3.6 fusion.28
  310.0 11.6 %reshape.70 = bf16[20,64,16,72]{3,2,1,0:T(8,128)(2,1)} reshape(bf16[20,64,1152]{2,1,0:T(8,128)(2,1)} %get-tuple-element.10) | data formatting | bytes 5898240 | tf_op jit(solution)/shard_map/reshape | solution.py:41
  321.6 11.6 %reshape.71 = bf16[20,64,16,72]{3,2,1,0:T(8,128)(2,1)} reshape(bf16[20,64,1152]{2,1,0:T(8,128)(2,1)} %get-tuple-element.9) | data formatting | bytes 5898240 | tf_op jit(solution)/shard_map/reshape | solution.py:38
  333.2 11.6 %reshape.69 = bf16[20,64,16,72]{3,2,1,0:T(8,128)(2,1)} reshape(bf16[20,64,1152]{2,1,0:T(8,128)(2,1)} %get-tuple-element.8) | data formatting | bytes 5898240 | tf_op jit(solution)/shard_map/reshape | solution.py:44
  344.8 28.2 %fusion.8 = f32[16,64,20,20]{3,2,1,0:T(8,128)} fusion(bf16[20,64,16,72]{3,2,1,0:T(8,128)(2,1)} %reshape.71, bf16[20,64,16,72]{3,2,1,0:T(8,128)(2,1)} %reshape.70), kind=kOutput, calls=%fused_computation.11 | convolution fusion | flops 58982400 | bytes 7536640 | tf_op jit(solution)/shard_map/fshd,gshd->hfgs/dot_general | solution.py:47
  373.0 16.4 %fusion.29 = (f32[16,20,64]{1,2,0:T(8,128)S(1)}, f32[16,20,20,64]{1,2,3,0:T(8,128)}) fusion(f32[16,64,20,20]{3,2,1,0:T(8,128)} %fusion.8, pred[20]{0:T(512)(128)(4,1)S(1)} %iota_compare_fusion), kind=kOutput, calls=%fused_computation.40 | output fusion | flops 2457619 | bytes 3358740 | tf_op jit(solution)/shard_map/sub | solution.py:52
  389.4 8.6 %convert_bitcast_fusion = bf16[20,64,16,72]{3,0,2,1:T(8,128)(2,1)S(1)} fusion(bf16[20,64,16,72]{3,2,1,0:T(8,128)(2,1)} %reshape.69, f32[16,20,20,64]{1,2,3,0:T(8,128)} %get-tuple-element.12, f32[16,20,64]{1,2,0:T(8,128)S(1)} %get-tuple-element.11), kind=kOutput, calls=%fused_computation.14 | convolution fusion | flops 61276160 | bytes 7618560 | tf_op jit(solution)/shard_map/hfgs,gshd->fshd/dot_general | solution.py:53
  398.0 3.4 copy.27
  401.4 9.0 %reshape.72 = bf16[20,64,1152]{2,1,0:T(8,128)(2,1)} reshape(bf16[20,64,16,72]{3,2,1,0:T(8,128)(2,1)} %copy.27) | data formatting | bytes 5898240 | tf_op jit(solution)/shard_map/reshape | solution.py:56
  410.4 4.6 all-to-all-start.1
  415.1 0.0 all-gather.7.cloned.1.call-done
  415.1 5.7 %reshape.78 = bf16[1152,1152,1]{1,0,2:T(8,128)(2,1)} reshape(bf16[128,9,1152]{2,1,0:T(8,128)(2,1)} %all-gather.7.cloned.1.call-done) | data formatting | bytes 5308416
  420.8 29.6 %all-to-all-done.1 = bf16[20,64,1152]{2,1,0:T(8,128)(2,1)} async-done(((bf16[20,64,1152]{2,1,0:T(8,128)(2,1)}), bf16[20,64,1152]{2,1,0:T(8,128)(2,1)}, u32[]{:S(2)}, u32[]{:S(2)}) %all-to-all-start.1) | async-done | bytes 2949152 | tf_op jit(solution)/shard_map/all_to_all | solution.py:57
  450.5 0.0 copy-start.1
  450.5 2.2 copy.28
  452.7 0.4 copy-done.1
  453.1 5.8 %fusion.21 = bf16[1,5,256,1152]{3,2,1,0:T(8,128)(2,1)} fusion(bf16[5,256,1152]{2,1,0:T(8,128)(2,1)S(1)} %bitcast.62, bf16[1152,1152,1]{1,0,2:T(8,128)(2,1)S(1)} %copy-done.1, bf16[1,5,256,1152]{3,2,1,0:T(8,128)(2,1)S(1)} %copy-done, f32[5]{0:T(128)S(1)} %compare_convert_fusion, f32[1152]{0:T(1024)S(1)} %get-tuple-element.5), kind=kOutput, calls=%fused_computation.29 | convolution fusion | flops 3404759040 | bytes 11506196 | tf_op jit(solution)/shard_map/dot_general | solution.py:64
  (7 shorter events, 0.1 us)
Async XLA Ops:
  6.5 6.0 %copy-start = (bf16[1,5,256,1152]{3,2,1,0:T(8,128)(2,1)S(1)}, bf16[1,5,256,1152]{3,2,1,0:T(8,128)(2,1)}, u32[]{:S(2)}) copy-start(bf16[1,5,256,1152]{3,2,1,0:T(8,128)(2,1)} %param.5) | copy-start | bytes 8847364
  6.5 5.9 %copy-start.2 = (f32[1,3,1152]{2,0,1:T(1,128)S(1)}, f32[1,3,1152]{2,0,1:T(1,128)}, u32[]{:S(2)}) copy-start(f32[1,3,1152]{2,0,1:T(1,128)} %param.6) | copy-start | bytes 41476
  6.5 77.2 %all-gather.5.cloned.1.call-start = ((), (), s32[]{:S(2)}) async-start(), calls=%async_computation.2 | async-start | bytes 9510912 | tf_op jit(solution)/shard_map/all_gather | solution.py:33
  128.3 171.1 %all-to-all-start = ((bf16[5,256,3456]{2,0,1:T(8,128)(2,1)}), bf16[5,256,3456]{2,0,1:T(8,128)(2,1)}, u32[]{:S(2)}, u32[]{:S(2)}) async-start(bf16[5,256,3456]{2,0,1:T(8,128)(2,1)} %copy.20), calls=%async_computation | async-start | bytes 28311552 | tf_op jit(solution)/shard_map/all_to_all | solution.py:37
  134.8 280.3 %all-gather.7.cloned.1.call-start = ((), (), s32[]{:S(2)}) async-start(), calls=%async_computation.3 | async-start | bytes 4755456 | tf_op jit(solution)/shard_map/all_gather | solution.py:62
  410.4 40.0 %all-to-all-start.1 = ((bf16[20,64,1152]{2,1,0:T(8,128)(2,1)}), bf16[20,64,1152]{2,1,0:T(8,128)(2,1)}, u32[]{:S(2)}, u32[]{:S(2)}) async-start(bf16[20,64,1152]{2,1,0:T(8,128)(2,1)} %reshape.72), calls=%async_computation.1 | async-start | bytes 5898240 | tf_op jit(solution)/shard_map/all_to_all | solution.py:57
  450.5 2.6 copy-start.1
Sparse Core Ops, SparseCore 0:
  10.4 73.3 all-gather.4
  138.7 69.1 all-gather.6
where the time goes:
time: 470 us; the launch traced here: 466 us
  waiting for transfers between devices  262 us (56%)
  local copies, waits for them, and re-layouts  92.8 us (20%)
  matrix products  60.5 us (13%)
  other arithmetic  24.4 us (5%)
  between operations  14.4 us (3%)
  starting transfers between devices  11.5 us (2%)
    all_to_all x1, waiting for transfers between devices, on_device(): lax.all_to_all(qkv_rows, 'grp', split_axis=1, concat_axis=0, tiled=True)  163 us
    all_gather x1, waiting for transfers between devices, on_device(): lax.all_gather(qkv_weight, ('clip', 'grp'), axis=1, tiled=True)  68.5 us
    all_to_all x1, waiting for transfers between devices, on_device(): lax.all_to_all(mixed, 'grp', split_axis=0, concat_axis=1, tiled=True)  29.6 us
    dot_general x1, matrix products, on_device(): jnp.einsum('fshd,gshd->hfgs', query_heads, key_heads, preferred_element_t...  28.2 us
    unnamed x8, local copies, waits for them, and re-layouts  19.2 us
    dot_general x1, matrix products, on_device(): jnp.dot(frame_rows, lax.all_gather(qkv_weight, ('clip', 'grp'), axis=1, t...  18 us
    sub x1, other arithmetic, on_device(): attn_weights = jax.nn.softmax(scores, axis=2).astype(jnp.bfloat16)  16.4 us
    reshape x1, local copies, waits for them, and re-layouts, on_device(): qkv_rows = qkv_rows.reshape(own_frames, frame_tokens, 3 * model_width)  13.5 us
  transfers between devices with their start and end apart: 4, of which 3 were waited for; matrix products, arithmetic and copies ran while one was open for 27% of the time, Pallas kernels for 0%

commit v1 on v0

v1 whole, which is shorter than its diff:
```python
import functools

import jax
import jax.numpy as jnp
from jax import lax
from jax.experimental import pallas as pl
from jax.experimental.pallas import tpu as pltpu
from jax.sharding import PartitionSpec as P

HEADS = 16
NT = (((1,), (1,)), ((), ()))
NN = (((1,), (0,)), ((), ()))
CHUNKS = ((0, 32), (32, 32))


def block_kernel(granules, x_ref, w_ref, table, bias, gate, o_ref, xm, qkv, mixed, proj):
    width = x_ref.shape[-1]
    head = width // HEADS
    low = lax.broadcasted_iota(jnp.int32, (8, width), 0) < 4

    def frame(f, g):
        return x_ref[f // 5, f % 5, pl.ds(pl.multiple_of(8 * g, 8), 8), :].astype(jnp.float32)

    def normal(x):
        mu = jnp.mean(x, axis=-1, keepdims=True)
        c = x - mu
        var = jnp.mean(c * c, axis=-1, keepdims=True)
        return c * lax.rsqrt(var + 1e-6) * (1.0 + table[1:2, :]) + table[0:1, :]

    def interleave(a, b):
        lo = jnp.where(low, a, pltpu.roll(b, 4, 0))
        hi = jnp.where(low, pltpu.roll(a, 4, 0), b)
        return lo, hi

    def norm_step(g, carry):
        base = g * 160
        for i in range(5):
            lo0, hi0 = interleave(normal(frame(4 * i, g)), normal(frame(4 * i + 1, g)))
            lo1, hi1 = interleave(normal(frame(4 * i + 2, g)), normal(frame(4 * i + 3, g)))
            xm[pl.ds(pl.multiple_of(base + 16 * i, 16), 16), :] = jnp.concatenate([lo0, lo1], 0).astype(jnp.bfloat16)
            xm[pl.ds(pl.multiple_of(base + 80 + 16 * i, 16), 16), :] = jnp.concatenate([hi0, hi1], 0).astype(jnp.bfloat16)
        return carry

    lax.fori_loop(0, granules, norm_step, 0)

    for c in range(9):
        part = slice(384 * c, 384 * c + 384)
        qkv[:, part] = lax.dot_general(xm[...], w_ref[part, :], NT, preferred_element_type=jnp.float32).astype(jnp.bfloat16)

    column = lax.broadcasted_iota(jnp.int32, (80, 256), 1)
    scale = head ** -0.5

    def attend(t, carry):
        r = pl.ds(pl.multiple_of(80 * t, 16), 80)
        both = jnp.concatenate([bias[...], bias[...]], 0)
        rest = None
        for j in range(8):
            q = qkv[r, 128 * j:128 * j + 256]
            k = qkv[r, width + 128 * j:width + 128 * j + 256]
            v = qkv[r, 2 * width + 128 * j:2 * width + 128 * j + 256]
            first = (column >= 16 * j) & (column < 16 * j + 72)
            second = (column >= 16 * j + 72) & (column < 16 * j + 144)
            fa = first.astype(jnp.float32).astype(jnp.bfloat16)
            fb = second.astype(jnp.float32).astype(jnp.bfloat16)
            qq = jnp.concatenate([q * fa, q * fb], 0)
            s = lax.dot_general(qq, k, NT, preferred_element_type=jnp.float32) * scale + both
            m = jnp.max(s, axis=-1, keepdims=True)
            p = jnp.exp(s - m)
            p = (p / jnp.sum(p, axis=-1, keepdims=True)).astype(jnp.bfloat16)
            o = lax.dot_general(p, v, NN, preferred_element_type=jnp.float32)
            o = jnp.where(first, o[:80], jnp.where(second, o[80:], 0.0))
            done = o[:, :128] if rest is None else o[:, :128] + rest
            mixed[r, 128 * j:128 * j + 128] = done.astype(jnp.bfloat16)
            rest = o[:, 128:]
        mixed[r, 1024:1152] = rest.astype(jnp.bfloat16)
        return carry

    lax.fori_loop(0, 2 * granules, attend, 0)

    for c in range(3):
        part = slice(384 * c, 384 * c + 384)
        from_row = 3 * width + 384 * c
        proj[:, part] = lax.dot_general(mixed[...], w_ref[from_row:from_row + 384, :], NT, preferred_element_type=jnp.float32)

    def finish(g, carry):
        base = g * 160
        at = pl.ds(pl.multiple_of(8 * g, 8), 8)
        for i in range(10):
            lo = proj[pl.ds(pl.multiple_of(base + 8 * i, 8), 8), :]
            hi = proj[pl.ds(pl.multiple_of(base + 80 + 8 * i, 8), 8), :]
            for f, y in zip((2 * i, 2 * i + 1), interleave(lo, hi)):
                o_ref[f // 5, f % 5, at, :] = (frame(f, g) + gate[f] * y).astype(jnp.bfloat16)
        return carry

    lax.fori_loop(0, granules, finish, 0)


def block(x, w, table, bias, gate, start, size):
    groups, frames, _, width = x.shape
    granules = size // 8
    rows = 160 * granules
    vmem = pl.BlockSpec(memory_space=pltpu.VMEM)
    return pl.pallas_call(
        functools.partial(block_kernel, granules),
        grid=(1,),
        in_specs=[pl.BlockSpec((groups, frames, size, width), lambda i: (0, 0, start // size, 0)), vmem, vmem, vmem, vmem],
        out_specs=pl.BlockSpec((groups, frames, size, width), lambda i: (0, 0, 0, 0)),
        out_shape=jax.ShapeDtypeStruct((groups, frames, size, width), jnp.bfloat16),
        scratch_shapes=[
            pltpu.VMEM((rows, width), jnp.bfloat16),
            pltpu.VMEM((rows, 3 * width), jnp.bfloat16),
            pltpu.VMEM((rows, width), jnp.bfloat16),
            pltpu.VMEM((rows, width), jnp.float32),
        ],
        compiler_params=pltpu.CompilerParams(vmem_limit_bytes=44 << 20),
        cost_estimate=pl.CostEstimate(flops=2 * rows * width * width * 5, bytes_accessed=rows * width * 8, transcendentals=rows * 1280),
    )(x, w, table, bias, gate)


def load_kernel(rows_ref, *refs):
    pieces, out, sems = refs[:16], refs[16], refs[17]
    copies = []
    for i, piece in enumerate(pieces):
        for r in range(4):
            at = pl.multiple_of(rows_ref[4 * i + r], 8)
            copies.append(pltpu.make_async_copy(piece.at[r], out.at[pl.ds(at, 72)], sems.at[4 * i + r]))
    for c in copies:
        c.start()
    for c in copies:
        c.wait()


def load(rows, pieces):
    width = pieces[0].shape[-1]
    return pl.pallas_call(
        load_kernel,
        grid_spec=pltpu.PrefetchScalarGridSpec(
            num_scalar_prefetch=1,
            grid=(1,),
            in_specs=[pl.BlockSpec(memory_space=pl.ANY)] * 16,
            out_specs=pl.BlockSpec(memory_space=pltpu.VMEM),
            scratch_shapes=[pltpu.SemaphoreType.DMA((64,))],
        ),
        out_shape=pltpu.VMEM((4 * width, width), jnp.bfloat16),
        compiler_params=pltpu.CompilerParams(vmem_limit_bytes=44 << 20),
    )(rows, *pieces)


def on_ring(axis, k):
    n = 4
    if axis == "y":
        return [(i, (i + k) % n) for i in range(n)]
    if axis == "z":
        return [(z * 8 + r, ((z + k) % n) * 8 + r) for z in range(n) for r in range(8)]
    if axis == "x":
        return [(z * 8 + x * 2 + c, z * 8 + ((x + k) % n) * 2 + c) for z in range(n) for x in range(n) for c in range(2)]
    return [(i, i ^ 1) for i in range(32)]


def send(value, axis, k=1):
    return lax.ppermute(value, "grp" if axis == "y" else "clip", on_ring(axis, k))


def weights(qkv_weight, out_weight):
    width = qkv_weight.shape[0]
    clip, y = lax.axis_index("clip"), lax.axis_index("grp")
    z, x, c = clip // 8, (clip // 2) % 4, clip % 2
    own = jnp.concatenate([qkv_weight.T, out_weight.T], 0)
    pieces = jnp.stack([own] + [send(own, "y", k) for k in (1, 2, 3)])
    pieces = jnp.take(pieces, (y - jnp.arange(4)) % 4, axis=0)
    other = send(pieces, "core")
    chip = jnp.take(jnp.stack([pieces, other]), (c + jnp.arange(2)) % 2, axis=0).reshape(8, 36, width)
    qkv_rows, out_rows = chip[:, :27].reshape(216, width), chip[:, 27:].reshape(72, width)
    half = jnp.where(c == 0, qkv_rows[:144], jnp.concatenate([qkv_rows[144:], out_rows], 0))
    a, b = half[:72], half[72:]
    ax = jnp.stack([a] + [send(a, "x", k) for k in (1, 2, 3)])
    bz = jnp.stack([b] + [send(b, "z", k) for k in (1, 2, 3)])
    az = [ax] + [send(ax, "z", k) for k in (1, 3, 2)]
    bx = [bz] + [send(bz, "x", k) for k in (1, 3, 2)]
    mine = az + bx
    pieces = mine + [send(t, "core") for t in mine]
    rows = []
    for core in (c, 1 - c):
        for kind in range(2):
            for k in (0, 1, 3, 2):
                for r in range(4):
                    zz, xx = ((z - k) % 4, (x - r) % 4) if kind == 0 else ((z - r) % 4, (x - k) % 4)
                    chip = 4 * zz + xx
                    first, second = (3 * chip, 3 * chip + 2) if kind == 0 else (3 * chip + 1, 48 + chip)
                    rows.append(72 * jnp.where(core == 0, first, second))
    return load(jnp.stack(rows).astype(jnp.int32), pieces)


def on_device(hidden, modulation, clip_frames, qkv_weight, out_weight):
    _, own_frames, tokens, width = hidden.shape
    table, length = modulation[0], clip_frames[0]
    parts = hidden[0].reshape(own_frames, 4, tokens // 4, width).transpose(1, 0, 2, 3)
    x = lax.all_to_all(parts, "grp", 0, 0, tiled=True)
    w = weights(qkv_weight, out_weight)
    live = jnp.arange(4 * own_frames) < length
    key = jnp.arange(16 * own_frames)
    bias = jnp.where((key[:, None] % 4 == key[None, :] % 4) & jnp.repeat(live, 4)[None, :], 0.0, -1e30).astype(jnp.float32)
    gate = live.astype(jnp.float32)[:, None, None] * table[2]
    outs = []
    for start, size in CHUNKS:
        o = block(x, w, table, bias, gate, start, size)
        outs.append(lax.all_to_all(o, "grp", 0, 0, tiled=True))
    out = jnp.concatenate(outs, 2)
    return out.transpose(1, 0, 2, 3).reshape(1, own_frames, tokens, width)


def solution(mesh):
    placed = (
        P("clip", "grp", None, None),
        P("clip", None, None),
        P("clip"),
        P(None, ("clip", "grp")),
        P(None, ("clip", "grp")),
    )
    return jax.shard_map(on_device, mesh=mesh, in_specs=placed, out_specs=P("clip", "grp", None, None), check_vma=False)
```

time: 470 us -> 208 us (0.44)
  waiting for transfers between devices: 262 us -> 65.5 us
  local copies, waits for them, and re-layouts: 92.8 us -> 18.1 us
  matrix products: 60.5 us -> 0 us
  Pallas kernels: 0 us -> 57.5 us
  blocking collectives: 0 us -> 24.2 us
  starting transfers between devices: 11.5 us -> 34.7 us
  other arithmetic: 24.4 us -> 6.69 us
  between operations: 14.4 us -> 1 us
    all_to_all x2, waiting for transfers between devices: 193 us -> 0.01 us  [the longest x1 0.01 us: on_device(): x = lax.all_to_all(parts, 'grp', 0, 0, tiled=True)]
    all_gather x2 -> x0, waiting for transfers between devices: 68.5 us -> none  [the longest x1 68.5 us: on_device(): lax.all_gather(qkv_weight, ('clip', 'grp'), axis=1, tiled=True)]
    ppermute x0 -> x24, waiting for transfers between devices: none -> 65.5 us  [send(): lax.ppermute(value, 'grp' if axis == 'y' else 'clip', on_ring(axis, k))]
    dot_general x4 -> x0, matrix products: 60.5 us -> none  [the longest x1 28.2 us: on_device(): jnp.einsum('fshd,gshd->hfgs', query_heads, key_heads, preferred_element_t...]
    pallas_call x0 -> x3, Pallas kernels: none -> 57.5 us  [the longest x2 52.2 us: block(): pl.pallas_call(functools.partial(block_kernel, granules), grid=(1,), in_s...]
    reshape x5 -> x2, local copies, waits for them, and re-layouts: 57.4 us -> 0.25 us  [the longest x1 0.17 us: weights(): chip[:, :27].reshape(216, width)]
    ppermute x0 -> x24, starting transfers between devices: none -> 26.4 us  [send(): lax.ppermute(value, 'grp' if axis == 'y' else 'clip', on_ring(axis, k))]
    all_to_all x0 -> x1, blocking collectives: none -> 24.2 us  [on_device(): outs.append(lax.all_to_all(o, 'grp', 0, 0, tiled=True))]
  transfers between devices with their start and end apart: 4 -> 26, of which waited for: 3 -> 12; matrix products, arithmetic and copies ran while one was open for 27% -> 4% of each run, Pallas kernels for 0% -> 15%
where the time goes in v1:
time: 208 us
  waiting for transfers between devices  65.5 us (31%)
  Pallas kernels  57.5 us (28%)
  starting transfers between devices  34.7 us (17%)
  blocking collectives  24.2 us (12%)
  local copies, waits for them, and re-layouts  18.1 us (9%)
  other arithmetic  6.69 us (3%)
    ppermute x24, waiting for transfers between devices, send(): lax.ppermute(value, 'grp' if axis == 'y' else 'clip', on_ring(axis, k))  65.5 us
    pallas_call x2, Pallas kernels, block(): pl.pallas_call(functools.partial(block_kernel, granules), grid=(1,), in_s...  52.2 us
    ppermute x24, starting transfers between devices, send(): lax.ppermute(value, 'grp' if axis == 'y' else 'clip', on_ring(axis, k))  26.4 us
    all_to_all x1, blocking collectives, on_device(): outs.append(lax.all_to_all(o, 'grp', 0, 0, tiled=True))  24.2 us
    unnamed x27, local copies, waits for them, and re-layouts  9 us
    pallas_call x1, Pallas kernels, load(): pl.pallas_call(load_kernel, grid_spec=pltpu.PrefetchScalarGridSpec(num_sc...  5.36 us
    all_to_all x1, starting transfers between devices, on_device(): outs.append(lax.all_to_all(o, 'grp', 0, 0, tiled=True))  4.54 us
  transfers between devices with their start and end apart: 26, of which 12 were waited for; matrix products, arithmetic and copies ran while one was open for 4% of the time, Pallas kernels for 15%

profile of v1, /device:TPU:0, one launch (start us, length us, event | category | flops | bytes accessed | tf_op | source)
XLA Modules:
  0.0 207.8 jit_solution(3667735113899081687)
XLA Ops:
  0.0 0.9 pad_maximum_fusion.4
  0.9 1.7 collective-permute-start
  2.7 2.9 %collective-permute-start.1 = (bf16[36,1152]{1,0:T(8,128)(2,1)S(1)}, bf16[36,1152]{1,0:T(8,128)(2,1)S(1)}, u32[]{:S(2)}, u32[]{:S(2)}) collective-permute-start(bf16[36,1152]{1,0:T(8,128)(2,1)S(1)} %pad_maximum_fusion.4), channel_id=1, source_target_pairs={{0,2},{1,3},{2,0},{3,1},{4,6},{5,7},{6,4},{7,5},{8,10},{9,11},{10,... | collective-permute-start | bytes 248840 | tf_op jit(solution)/shard_map/ppermute | solution.py:161
  5.6 1.3 collective-permute-start.2
  6.9 0.9 fusion.7
  8.1 1.8 collective-permute-done.1
  10.2 0.6 gather_fusion
  11.1 1.6 collective-permute-done.3
  12.8 0.7 gather_fusion.1
  14.1 0.7 slice_bitcast_fusion
  14.8 1.9 collective-permute-start.10
  16.7 3.6 %collective-permute-start.11 = (bf16[72,1152]{1,0:T(8,128)(2,1)}, bf16[72,1152]{1,0:T(8,128)(2,1)}, u32[]{:S(2)}, u32[]{:S(2)}) collective-permute-start(bf16[72,1152]{1,0:T(8,128)(2,1)} %get-tuple-element.7), channel_id=1, source_target_pairs={{0,64},{4,68},{8,72},{12,76},{16,80},{20,84},{24,88},{28,92},{32,9... | collective-permute-start | bytes 497672 | tf_op jit(solution)/shard_map/ppermute | solution.py:161
  20.3 1.0 collective-permute-start.12
  21.3 3.7 %copy.11 = bf16[5,4,64,1152]{3,2,0,1:T(8,128)(2,1)} copy(bf16[5,4,64,1152]{3,2,1,0:T(8,128)(2,1)} %bitcast.106) | data formatting | bytes 5898240 | tf_op jit(solution)/shard_map/reshape;squeeze | solution.py:197
  25.0 3.8 %all-to-all-start = ((bf16[4,5,64,1152]{3,2,1,0:T(8,128)(2,1)}), bf16[4,5,64,1152]{3,2,1,0:T(8,128)(2,1)S(1)}, u32[]{:S(2)}, u32[]{:S(2)}) async-start(bf16[4,5,64,1152]{3,2,1,0:T(8,128)(2,1)} %bitcast.105), calls=%async_computation | async-start | bytes 5898240 | tf_op jit(solution)/shard_map/all_to_all | solution.py:198
  28.9 1.5 collective-permute-start.4
  30.4 1.2 pad_maximum_fusion.2.refs_4_
  31.5 1.6 collective-permute-start.13
  33.1 1.7 collective-permute-start.14
  34.9 1.5 collective-permute-start.15
  36.6 2.1 %collective-permute-start.5 = (bf16[72,1152]{1,0:T(8,128)(2,1)S(1)}, bf16[72,1152]{1,0:T(8,128)(2,1)S(1)}, u32[]{:S(2)}, u32[]{:S(2)}) collective-permute-start(bf16[72,1152]{1,0:T(8,128)(2,1)S(1)} %get-tuple-element.8), channel_id=1, source_target_pairs={{0,16},{4,20},{8,24},{12,28},{16,0},{20,4},{24,8},{28,12},{32,48},... | collective-permute-start | bytes 497672 | tf_op jit(solution)/shard_map/ppermute | solution.py:161
  38.7 29.7 %collective-permute-done.5 = bf16[72,1152]{1,0:T(8,128)(2,1)S(1)} collective-permute-done((bf16[72,1152]{1,0:T(8,128)(2,1)S(1)}, bf16[72,1152]{1,0:T(8,128)(2,1)S(1)}, u32[]{:S(2)}, u32[]{:S(2)}) %collective-permute-start.5) | collective-permute-done | bytes 165920 | tf_op jit(solution)/shard_map/ppermute | solution.py:161
  68.4 0.7 collective-permute-start.6
  69.2 4.6 %collective-permute-done.6 = bf16[72,1152]{1,0:T(8,128)(2,1)S(1)} collective-permute-done((bf16[72,1152]{1,0:T(8,128)(2,1)S(1)}, bf16[72,1152]{1,0:T(8,128)(2,1)S(1)}, u32[]{:S(2)}, u32[]{:S(2)}) %collective-permute-start.6) | collective-permute-done | bytes 165920 | tf_op jit(solution)/shard_map/ppermute | solution.py:161
  73.8 1.0 pad_maximum_fusion.1.refs_0_
  74.7 1.0 collective-permute-start.7
  75.7 2.2 %collective-permute-start.8 = (bf16[4,72,1152]{2,1,0:T(8,128)(2,1)}, bf16[4,72,1152]{2,1,0:T(8,128)(2,1)}, u32[]{:S(2)}, u32[]{:S(2)}) collective-permute-start(bf16[4,72,1152]{2,1,0:T(8,128)(2,1)} %pad_maximum_fusion.1.refs_0_), channel_id=1, source_target_pairs={{0,96},{4,100},{8,104},{12,108},{16,112},{20,116},{24,120},{28,124... | collective-permute-start | bytes 1990664 | tf_op jit(solution)/shard_map/ppermute | solution.py:161
  78.1 0.7 copy-done.4
  79.1 0.9 copy-done.6
  80.8 0.8 stack.311.rows_ref
  81.6 22.8 %collective-permute-done.7.refs_1_ = bf16[4,72,1152]{2,1,0:T(8,128)(2,1)} collective-permute-done((bf16[4,72,1152]{2,1,0:T(8,128)(2,1)}, bf16[4,72,1152]{2,1,0:T(8,128)(2,1)}, u32[]{:S(2)}, u32[]{:S(2)}) %collective-permute-start.7) | collective-permute-done | bytes 663584 | tf_op jit(solution)/shard_map/ppermute | solution.py:161
  104.5 0.5 collective-permute-start.23
  106.0 0.8 collective-permute-done.22.refs_14_
  106.8 0.9 collective-permute-done.23.refs_15_
  107.7 0.9 collective-permute-done.17.refs_9_
  108.7 0.9 collective-permute-done.18.refs_10_
  109.6 0.9 collective-permute-done.19.refs_11_
  110.6 0.8 copy-done.11
  111.4 5.4 %shard_map.55.w_ref = bf16[4608,1152]{1,0:T(8,128)(2,1)S(1)} custom-call(s32[64]{0:T(128)} %stack.311.rows_ref, bf16[4,72,1152]{2,1,0:T(8,128)(2,1)} %pad_maximum_fusion.1.refs_0_, bf16[4,72,1152]{2,1,0:T(8,128)(2,1)} %collective-permute-done.7.refs_1_, bf16[4,72,1152]{2,1,0:T(8,128)(2,1)} %collective-permute-done.8.refs_2_, ...), custom_call_target="tpu_custom_call" | custom-call | tf_op jit(solution)/shard_map/pallas_call | solution.py:135
  116.8 4.0 %copy-done = bf16[4608,1152]{1,0:T(8,128)(2,1)} copy-done((bf16[4608,1152]{1,0:T(8,128)(2,1)}, bf16[4608,1152]{1,0:T(8,128)(2,1)S(1)}, u32[]{:S(2)}) %copy-start) | copy-done | bytes 10616856
  120.8 26.1 %shard_map.56 = bf16[4,5,32,1152]{3,2,1,0:T(8,128)(2,1)S(1)} custom-call(bf16[4,5,64,1152]{3,2,1,0:T(8,128)(2,1)S(1)} %all-to-all-done.x_ref, bf16[4608,1152]{1,0:T(8,128)(2,1)} %copy-done, f32[3,1152]{1,0:T(4,128)S(1)} %bitcast.103, f32[80,80]{1,0:T(8,128)S(1)} %and_select_fusion.bias, f32[20,1,1152]{2,1,0:T(1,128)S(1)} %broadcast_multiply_fusion.gate), custom_call_target="tpu_custom_call" | custom-call | flops 8493465600 | bytes 5898240 | tf_op jit(solution)/shard_map/pallas_call | solution.py:103
  146.9 1.2 copy-done.1
  148.1 4.5 %all-to-all-start.1 = ((bf16[4,5,32,1152]{3,2,1,0:T(8,128)(2,1)}), bf16[4,5,32,1152]{3,2,1,0:T(8,128)(2,1)}, u32[]{:S(2)}, u32[]{:S(2)}) async-start(bf16[4,5,32,1152]{3,2,1,0:T(8,128)(2,1)} %copy-done.1), calls=%async_computation.1 | async-start | bytes 2949120 | tf_op jit(solution)/shard_map/all_to_all | solution.py:207
  152.6 26.1 %shard_map.57 = bf16[4,5,32,1152]{3,2,1,0:T(8,128)(2,1)S(1)} custom-call(bf16[4,5,64,1152]{3,2,1,0:T(8,128)(2,1)S(1)} %all-to-all-done.x_ref, bf16[4608,1152]{1,0:T(8,128)(2,1)} %copy-done, f32[3,1152]{1,0:T(4,128)S(1)} %bitcast.104, f32[80,80]{1,0:T(8,128)S(1)} %and_select_fusion.bias, f32[20,1,1152]{2,1,0:T(1,128)S(1)} %broadcast_multiply_fusion.gate), custom_call_target="tpu_custom_call" | custom-call | flops 8493465600 | bytes 5898240 | tf_op jit(solution)/shard_map/pallas_call | solution.py:103
  178.8 1.1 copy-done.2
  179.9 24.2 %all_to_all.15 = bf16[4,5,32,1152]{3,2,1,0:T(8,128)(2,1)S(1)} all-to-all(bf16[4,5,32,1152]{3,2,1,0:T(8,128)(2,1)} %copy-done.2), channel_id=1, replica_groups=mesh['clip'=32,'grp'=4] {'grp'}, dimensions={0} | all-to-all | bytes 2949120 | tf_op jit(solution)/shard_map/all_to_all | solution.py:207
  204.1 1.8 maximum_bitcast_fusion
  205.9 1.9 copy.7
  (73 shorter events, 3.3 us)
Async XLA Ops:
  0.9 7.2 %collective-permute-start = (bf16[36,1152]{1,0:T(8,128)(2,1)S(1)}, bf16[36,1152]{1,0:T(8,128)(2,1)S(1)}, u32[]{:S(2)}, u32[]{:S(2)}) collective-permute-start(bf16[36,1152]{1,0:T(8,128)(2,1)S(1)} %pad_maximum_fusion.4), channel_id=1, source_target_pairs={{0,1},{1,2},{2,3},{3,0},{4,5},{5,6},{6,7},{7,4},{8,9},{9,10},{10,1... | collective-permute-start | bytes 248840 | tf_op jit(solution)/shard_map/ppermute | solution.py:161
  2.7 7.3 %collective-permute-start.1 = (bf16[36,1152]{1,0:T(8,128)(2,1)S(1)}, bf16[36,1152]{1,0:T(8,128)(2,1)S(1)}, u32[]{:S(2)}, u32[]{:S(2)}) collective-permute-start(bf16[36,1152]{1,0:T(8,128)(2,1)S(1)} %pad_maximum_fusion.4), channel_id=1, source_target_pairs={{0,2},{1,3},{2,0},{3,1},{4,6},{5,7},{6,4},{7,5},{8,10},{9,11},{10,... | collective-permute-start | bytes 248840 | tf_op jit(solution)/shard_map/ppermute | solution.py:161
  5.6 4.6 %collective-permute-start.2 = (bf16[36,1152]{1,0:T(8,128)(2,1)S(1)}, bf16[36,1152]{1,0:T(8,128)(2,1)S(1)}, u32[]{:S(2)}, u32[]{:S(2)}) collective-permute-start(bf16[36,1152]{1,0:T(8,128)(2,1)S(1)} %pad_maximum_fusion.4), channel_id=1, source_target_pairs={{0,3},{1,0},{2,1},{3,2},{4,7},{5,4},{6,5},{7,6},{8,11},{9,8},{10,9... | collective-permute-start | bytes 248840 | tf_op jit(solution)/shard_map/ppermute | solution.py:161
  10.9 1.8 collective-permute-start.3
  14.8 15.5 %collective-permute-start.10 = (bf16[72,1152]{1,0:T(8,128)(2,1)}, bf16[72,1152]{1,0:T(8,128)(2,1)}, u32[]{:S(2)}, u32[]{:S(2)}) collective-permute-start(bf16[72,1152]{1,0:T(8,128)(2,1)} %get-tuple-element.7), channel_id=1, source_target_pairs={{0,32},{4,36},{8,40},{12,44},{16,48},{20,52},{24,56},{28,60},{32,6... | collective-permute-start | bytes 497672 | tf_op jit(solution)/shard_map/ppermute | solution.py:161
  16.7 13.6 %collective-permute-start.11 = (bf16[72,1152]{1,0:T(8,128)(2,1)}, bf16[72,1152]{1,0:T(8,128)(2,1)}, u32[]{:S(2)}, u32[]{:S(2)}) collective-permute-start(bf16[72,1152]{1,0:T(8,128)(2,1)} %get-tuple-element.7), channel_id=1, source_target_pairs={{0,64},{4,68},{8,72},{12,76},{16,80},{20,84},{24,88},{28,92},{32,9... | collective-permute-start | bytes 497672 | tf_op jit(solution)/shard_map/ppermute | solution.py:161
  20.3 10.0 %collective-permute-start.12 = (bf16[72,1152]{1,0:T(8,128)(2,1)}, bf16[72,1152]{1,0:T(8,128)(2,1)}, u32[]{:S(2)}, u32[]{:S(2)}) collective-permute-start(bf16[72,1152]{1,0:T(8,128)(2,1)} %get-tuple-element.7), channel_id=1, source_target_pairs={{0,96},{4,100},{8,104},{12,108},{16,112},{20,116},{24,120},{28,124... | collective-permute-start | bytes 497672 | tf_op jit(solution)/shard_map/ppermute | solution.py:161
  25.0 95.8 %all-to-all-start = ((bf16[4,5,64,1152]{3,2,1,0:T(8,128)(2,1)}), bf16[4,5,64,1152]{3,2,1,0:T(8,128)(2,1)S(1)}, u32[]{:S(2)}, u32[]{:S(2)}) async-start(bf16[4,5,64,1152]{3,2,1,0:T(8,128)(2,1)} %bitcast.105), calls=%async_computation | async-start | bytes 5898240 | tf_op jit(solution)/shard_map/all_to_all | solution.py:198
  28.8 51.9 %copy-start.12 = (f32[1,3,1152]{2,0,1:T(1,128)S(1)}, f32[1,3,1152]{2,0,1:T(1,128)}, u32[]{:S(2)}) copy-start(f32[1,3,1152]{2,0,1:T(1,128)} %param.6) | copy-start | bytes 41476
  28.9 7.7 %collective-permute-start.4 = (bf16[72,1152]{1,0:T(8,128)(2,1)S(1)}, bf16[72,1152]{1,0:T(8,128)(2,1)S(1)}, u32[]{:S(2)}, u32[]{:S(2)}) collective-permute-start(bf16[72,1152]{1,0:T(8,128)(2,1)S(1)} %get-tuple-element.8), channel_id=1, source_target_pairs={{0,8},{4,12},{8,16},{12,20},{16,24},{20,28},{24,0},{28,4},{32,40},... | collective-permute-start | bytes 497672 | tf_op jit(solution)/shard_map/ppermute | solution.py:161
  31.5 4.8 %copy-start.3 = (bf16[4,72,1152]{2,1,0:T(8,128)(2,1)}, bf16[4,72,1152]{2,1,0:T(8,128)(2,1)S(1)}, u32[]{:S(2)}) copy-start(bf16[4,72,1152]{2,1,0:T(8,128)(2,1)S(1)} %pad_maximum_fusion.2.refs_4_) | copy-start | bytes 1990660
  31.5 44.2 %collective-permute-start.13 = (bf16[4,72,1152]{2,1,0:T(8,128)(2,1)S(1)}, bf16[4,72,1152]{2,1,0:T(8,128)(2,1)}, u32[]{:S(2)}, u32[]{:S(2)}) collective-permute-start(bf16[4,72,1152]{2,1,0:T(8,128)(2,1)S(1)} %pad_maximum_fusion.2.refs_4_), channel_id=1, source_target_pairs={{0,8},{4,12},{8,16},{12,20},{16,24},{20,28},{24,0},{28,4},{32,40},... | collective-permute-start | bytes 1990664 | tf_op jit(solution)/shard_map/ppermute | solution.py:161
  33.1 44.9 %collective-permute-start.14 = (bf16[4,72,1152]{2,1,0:T(8,128)(2,1)S(1)}, bf16[4,72,1152]{2,1,0:T(8,128)(2,1)S(1)}, u32[]{:S(2)}, u32[]{:S(2)}) collective-permute-start(bf16[4,72,1152]{2,1,0:T(8,128)(2,1)S(1)} %pad_maximum_fusion.2.refs_4_), channel_id=1, source_target_pairs={{0,24},{4,28},{8,0},{12,4},{16,8},{20,12},{24,16},{28,20},{32,56},... | collective-permute-start | bytes 1990664 | tf_op jit(solution)/shard_map/ppermute | solution.py:161
  34.9 43.1 %collective-permute-start.15 = (bf16[4,72,1152]{2,1,0:T(8,128)(2,1)S(1)}, bf16[4,72,1152]{2,1,0:T(8,128)(2,1)S(1)}, u32[]{:S(2)}, u32[]{:S(2)}) collective-permute-start(bf16[4,72,1152]{2,1,0:T(8,128)(2,1)S(1)} %pad_maximum_fusion.2.refs_4_), channel_id=1, source_target_pairs={{0,16},{4,20},{8,24},{12,28},{16,0},{20,4},{24,8},{28,12},{32,48},... | collective-permute-start | bytes 1990664 | tf_op jit(solution)/shard_map/ppermute | solution.py:161
  36.4 41.7 %collective-permute-start.20 = (bf16[4,72,1152]{2,1,0:T(8,128)(2,1)S(1)}, bf16[4,72,1152]{2,1,0:T(8,128)(2,1)S(1)}, u32[]{:S(2)}, u32[]{:S(2)}) collective-permute-start(bf16[4,72,1152]{2,1,0:T(8,128)(2,1)S(1)} %pad_maximum_fusion.2.refs_4_), channel_id=1, source_target_pairs={{0,4},{4,0},{8,12},{12,8},{16,20},{20,16},{24,28},{28,24},{32,36},... | collective-permute-start | bytes 1990664 | tf_op jit(solution)/shard_map/ppermute | solution.py:161
  36.6 31.9 %collective-permute-start.5 = (bf16[72,1152]{1,0:T(8,128)(2,1)S(1)}, bf16[72,1152]{1,0:T(8,128)(2,1)S(1)}, u32[]{:S(2)}, u32[]{:S(2)}) collective-permute-start(bf16[72,1152]{1,0:T(8,128)(2,1)S(1)} %get-tuple-element.8), channel_id=1, source_target_pairs={{0,16},{4,20},{8,24},{12,28},{16,0},{20,4},{24,8},{28,12},{32,48},... | collective-permute-start | bytes 497672 | tf_op jit(solution)/shard_map/ppermute | solution.py:161
  68.4 5.3 %collective-permute-start.6 = (bf16[72,1152]{1,0:T(8,128)(2,1)S(1)}, bf16[72,1152]{1,0:T(8,128)(2,1)S(1)}, u32[]{:S(2)}, u32[]{:S(2)}) collective-permute-start(bf16[72,1152]{1,0:T(8,128)(2,1)S(1)} %get-tuple-element.8), channel_id=1, source_target_pairs={{0,24},{4,28},{8,0},{12,4},{16,8},{20,12},{24,16},{28,20},{32,56},... | collective-permute-start | bytes 497672 | tf_op jit(solution)/shard_map/ppermute | solution.py:161
  74.7 29.7 %collective-permute-start.7 = (bf16[4,72,1152]{2,1,0:T(8,128)(2,1)}, bf16[4,72,1152]{2,1,0:T(8,128)(2,1)}, u32[]{:S(2)}, u32[]{:S(2)}) collective-permute-start(bf16[4,72,1152]{2,1,0:T(8,128)(2,1)} %pad_maximum_fusion.1.refs_0_), channel_id=1, source_target_pairs={{0,32},{4,36},{8,40},{12,44},{16,48},{20,52},{24,56},{28,60},{32,6... | collective-permute-start | bytes 1990664 | tf_op jit(solution)/shard_map/ppermute | solution.py:161
  75.7 28.7 %collective-permute-start.8 = (bf16[4,72,1152]{2,1,0:T(8,128)(2,1)}, bf16[4,72,1152]{2,1,0:T(8,128)(2,1)}, u32[]{:S(2)}, u32[]{:S(2)}) collective-permute-start(bf16[4,72,1152]{2,1,0:T(8,128)(2,1)} %pad_maximum_fusion.1.refs_0_), channel_id=1, source_target_pairs={{0,96},{4,100},{8,104},{12,108},{16,112},{20,116},{24,120},{28,124... | collective-permute-start | bytes 1990664 | tf_op jit(solution)/shard_map/ppermute | solution.py:161
  78.0 0.8 copy-start.4
  78.0 27.0 %collective-permute-start.9 = (bf16[4,72,1152]{2,1,0:T(8,128)(2,1)}, bf16[4,72,1152]{2,1,0:T(8,128)(2,1)}, u32[]{:S(2)}, u32[]{:S(2)}) collective-permute-start(bf16[4,72,1152]{2,1,0:T(8,128)(2,1)} %pad_maximum_fusion.1.refs_0_), channel_id=1, source_target_pairs={{0,64},{4,68},{8,72},{12,76},{16,80},{20,84},{24,88},{28,92},{32,9... | collective-permute-start | bytes 1990664 | tf_op jit(solution)/shard_map/ppermute | solution.py:161
  78.0 1.1 copy-start.5
  78.0 27.1 %collective-permute-start.16 = (bf16[4,72,1152]{2,1,0:T(8,128)(2,1)}, bf16[4,72,1152]{2,1,0:T(8,128)(2,1)}, u32[]{:S(2)}, u32[]{:S(2)}) collective-permute-start(bf16[4,72,1152]{2,1,0:T(8,128)(2,1)} %pad_maximum_fusion.1.refs_0_), channel_id=1, source_target_pairs={{0,4},{4,0},{8,12},{12,8},{16,20},{20,16},{24,28},{28,24},{32,36},... | collective-permute-start | bytes 1990664 | tf_op jit(solution)/shard_map/ppermute | solution.py:161
  79.1 0.9 copy-start.6
  79.9 25.5 %collective-permute-start.21 = (bf16[4,72,1152]{2,1,0:T(8,128)(2,1)}, bf16[4,72,1152]{2,1,0:T(8,128)(2,1)}, u32[]{:S(2)}, u32[]{:S(2)}) collective-permute-start(bf16[4,72,1152]{2,1,0:T(8,128)(2,1)} %collective-permute-done.13.refs_5_), channel_id=1, source_target_pairs={{0,4},{4,0},{8,12},{12,8},{16,20},{20,16},{24,28},{28,24},{32,36},... | collective-permute-start | bytes 1990664 | tf_op jit(solution)/shard_map/ppermute | solution.py:161
  104.5 2.3 %collective-permute-start.22 = (bf16[4,72,1152]{2,1,0:T(8,128)(2,1)}, bf16[4,72,1152]{2,1,0:T(8,128)(2,1)S(1)}, u32[]{:S(2)}, u32[]{:S(2)}) collective-permute-start(bf16[4,72,1152]{2,1,0:T(8,128)(2,1)} %copy-done.4), channel_id=1, source_target_pairs={{0,4},{4,0},{8,12},{12,8},{16,20},{20,16},{24,28},{28,24},{32,36},... | collective-permute-start | bytes 1990664 | tf_op jit(solution)/shard_map/ppermute | solution.py:161
  104.5 3.3 %collective-permute-start.23 = (bf16[4,72,1152]{2,1,0:T(8,128)(2,1)}, bf16[4,72,1152]{2,1,0:T(8,128)(2,1)S(1)}, u32[]{:S(2)}, u32[]{:S(2)}) collective-permute-start(bf16[4,72,1152]{2,1,0:T(8,128)(2,1)} %copy-done.5), channel_id=1, source_target_pairs={{0,4},{4,0},{8,12},{12,8},{16,20},{20,16},{24,28},{28,24},{32,36},... | collective-permute-start | bytes 1990664 | tf_op jit(solution)/shard_map/ppermute | solution.py:161
  105.0 3.7 %collective-permute-start.17 = (bf16[4,72,1152]{2,1,0:T(8,128)(2,1)}, bf16[4,72,1152]{2,1,0:T(8,128)(2,1)S(1)}, u32[]{:S(2)}, u32[]{:S(2)}) collective-permute-start(bf16[4,72,1152]{2,1,0:T(8,128)(2,1)} %collective-permute-done.7.refs_1_), channel_id=1, source_target_pairs={{0,4},{4,0},{8,12},{12,8},{16,20},{20,16},{24,28},{28,24},{32,36},... | collective-permute-start | bytes 1990664 | tf_op jit(solution)/shard_map/ppermute | solution.py:161
  105.1 4.6 %collective-permute-start.18 = (bf16[4,72,1152]{2,1,0:T(8,128)(2,1)}, bf16[4,72,1152]{2,1,0:T(8,128)(2,1)S(1)}, u32[]{:S(2)}, u32[]{:S(2)}) collective-permute-start(bf16[4,72,1152]{2,1,0:T(8,128)(2,1)} %collective-permute-done.8.refs_2_), channel_id=1, source_target_pairs={{0,4},{4,0},{8,12},{12,8},{16,20},{20,16},{24,28},{28,24},{32,36},... | collective-permute-start | bytes 1990664 | tf_op jit(solution)/shard_map/ppermute | solution.py:161
  105.5 5.1 %collective-permute-start.19 = (bf16[4,72,1152]{2,1,0:T(8,128)(2,1)}, bf16[4,72,1152]{2,1,0:T(8,128)(2,1)S(1)}, u32[]{:S(2)}, u32[]{:S(2)}) collective-permute-start(bf16[4,72,1152]{2,1,0:T(8,128)(2,1)} %collective-permute-done.9.refs_3_), channel_id=1, source_target_pairs={{0,4},{4,0},{8,12},{12,8},{16,20},{20,16},{24,28},{28,24},{32,36},... | collective-permute-start | bytes 1990664 | tf_op jit(solution)/shard_map/ppermute | solution.py:161
  106.8 3.8 %copy-start.7 = (bf16[4,72,1152]{2,1,0:T(8,128)(2,1)}, bf16[4,72,1152]{2,1,0:T(8,128)(2,1)S(1)}, u32[]{:S(2)}) copy-start(bf16[4,72,1152]{2,1,0:T(8,128)(2,1)S(1)} %collective-permute-done.22.refs_14_) | copy-start | bytes 1990660
  107.7 2.9 %copy-start.8 = (bf16[4,72,1152]{2,1,0:T(8,128)(2,1)}, bf16[4,72,1152]{2,1,0:T(8,128)(2,1)S(1)}, u32[]{:S(2)}) copy-start(bf16[4,72,1152]{2,1,0:T(8,128)(2,1)S(1)} %collective-permute-done.23.refs_15_) | copy-start | bytes 1990660
  108.7 1.9 copy-start.9
  109.6 1.0 copy-start.10
  110.6 0.8 copy-start.11
  116.8 4.0 %copy-start = (bf16[4608,1152]{1,0:T(8,128)(2,1)}, bf16[4608,1152]{1,0:T(8,128)(2,1)S(1)}, u32[]{:S(2)}) copy-start(bf16[4608,1152]{1,0:T(8,128)(2,1)S(1)} %shard_map.55.w_ref) | copy-start | bytes 31850500
  146.9 1.2 copy-start.1
  148.1 31.8 %all-to-all-start.1 = ((bf16[4,5,32,1152]{3,2,1,0:T(8,128)(2,1)}), bf16[4,5,32,1152]{3,2,1,0:T(8,128)(2,1)}, u32[]{:S(2)}, u32[]{:S(2)}) async-start(bf16[4,5,32,1152]{3,2,1,0:T(8,128)(2,1)} %copy-done.1), calls=%async_computation.1 | async-start | bytes 2949120 | tf_op jit(solution)/shard_map/all_to_all | solution.py:207
  178.8 1.1 copy-start.2
